TPU v7x, 512 devices: a whole 4x8x8 slice. The times are simulated.
512 devices in a mesh: pages: 16 (over y, core), row: 8 (over z), col: 4 (over x).
Axes of the slice: x: 4, y: 8, z: 8, core: 2. Of those that a mesh axis runs over, the one named last changes fastest.
Arguments:
- residual: bfloat16 [512, 2, 2048], P('pages', None, ('row', 'col')), may hold values from -6 to 6
- fresh_qkv: bfloat16 [512, 2, 3, 2048], P('pages', None, None, 'col'), may hold values from -27 to 27
- prefix_pages: bfloat16 [256, 2, 128, 2048], P('pages', None, 'row', 'col'), may hold values from -6 to 6
- tail_pages: bfloat16 [512, 2, 128, 2048], P('pages', None, 'row', 'col'), may hold values from -6 to 6
- prefix_item: int32 [256], replicated, may hold values from 0 to 255, as said below
- tail_item: int32 [512], replicated, may hold values from 0 to 511, as said below
- prefix_length: int32 [32], replicated, may hold values from 1 to 1024, 20480 in all
- tail_length: int32 [512], replicated, may hold values from 1 to 128, 40960 in all
- out_weight: bfloat16 [2048, 2048], P('col', 'row'), may hold values from -0.125 to 0.125
- out_bias: bfloat16 [2048], P(('row', 'col')), may hold values from -4 to 4
- mlp_gain: bfloat16 [2048], P('row'), may hold values from 0.25 to 1.75
- mlp_shift: bfloat16 [2048], P('row'), may hold values from -4 to 4
- up_weight: bfloat16 [2048, 8192], P('row', 'col'), may hold values from -0.125 to 0.125
- up_bias: bfloat16 [8192], P(('col', 'row')), may hold values from -4 to 4
- down_weight: bfloat16 [8192, 2048], P('col', 'row'), may hold values from -0.0625 to 0.0625
- down_bias: bfloat16 [2048], P(('row', 'col')), may hold values from -4 to 4
- next_gain: bfloat16 [2048], P('row'), may hold values from 0.25 to 1.75
- next_shift: bfloat16 [2048], P('row'), may hold values from -4 to 4
- score_weight: bfloat16 [2048], P('row'), may hold values from -0.125 to 0.125
- qkv_weight: bfloat16 [2048, 6144], P('row', 'col'), may hold values from -0.125 to 0.125
- qkv_bias: bfloat16 [6144], P(('col', 'row')), may hold values from -4 to 4
Outputs:
- layer_out: bfloat16 [512, 2, 2048], P('pages', None, ('row', 'col'))
- score_out: float32 [512, 2], P('pages')
- projected_next: bfloat16 [512, 2, 6144], P('pages', None, ('col', 'row'))
Inputs may be any that keep to these rules, and one draw needn't show every extreme that they name: `prefix_item`: each of the 256 prompt pages is held by exactly one slot; slot h * 16 + g + k (k < 1) holds a page of one of the prompts g * 2 to (g + 1) * 2 - 1. `tail_item`: each continuation's tail is held by exactly one slot; slot h * 32 + g * 2 + k (k < 2) holds the tail of one of the continuations g * 32 to (g + 1) * 32 - 1. `prefix_length`: some prompt has exactly 1024 cached tokens. `tail_length`: some continuation has exactly 128 tail tokens.
All inputs are finite; a program needn't handle non-finite values.
Results may differ from a plain program's by a relative error of at most 0.023.
Values may be sent and summed in bfloat16 or wider, within the bound.
No kernel may reach another device: no remote copies, remote signals or barrier semaphores. Data moves between devices by JAX's collectives and lax.ppermute only.
A program may use at most 64 MiB of HBM per device.

v0:
```python
import math
import jax
import jax.numpy as jnp
from jax import lax
from jax.sharding import PartitionSpec as P

D = 2048
H = 16
HD = 128
PAGE = 128
MAXPAGES = 8
CONT = 16
masked_score = -1e30
norm_eps = 1e-05


def combined_all(shard, axis, combine):
    everything = jax.tree.map(lambda part: lax.all_gather(part, axis), shard)
    first = jax.tree.map(lambda part: part[0], everything)

    def step(k, so_far):
        return combine(so_far, jax.tree.map(lambda part: part[k], everything))

    return lax.fori_loop(1, lax.axis_size(axis), step, first)


def head_slopes(first_head, how_many):
    head_index = first_head + jnp.arange(how_many, dtype=jnp.int32)
    return jnp.exp2(-8.0 * (head_index + 1).astype(jnp.float32) / H)


def slot_partials(queries, page_keys, page_values, usable, offset, slopes):
    scores = jnp.einsum(
        "sqhd,skhd->sqhk", queries, page_keys, preferred_element_type=jnp.float32
    ) / math.sqrt(HD)
    scores = scores + slopes[None, None, :, None] * offset[:, :, None, :]
    usable_full = usable[:, :, None, :]
    scores = jnp.where(usable_full, scores, masked_score)
    maxima = jnp.max(scores, axis=3)
    weights = jnp.where(usable_full, jnp.exp(scores - maxima[..., None]), 0.0)
    totals = jnp.sum(weights, axis=3)
    outputs = jnp.einsum(
        "sqhk,skhd->sqhd", weights, page_values.astype(jnp.float32), precision=lax.Precision.HIGHEST
    )
    return (maxima, totals, outputs)


def merge_pair(left_part, right_part):
    left_max, left_total, left_out = left_part
    right_max, right_total, right_out = right_part
    joined = jnp.maximum(left_max, right_max)
    left_scale = jnp.exp(left_max - joined)
    right_scale = jnp.exp(right_max - joined)
    return (
        joined,
        left_scale * left_total + right_scale * right_total,
        left_scale[..., None] * left_out + right_scale[..., None] * right_out,
    )


def fold_sources(maxima, totals, outputs):
    joined = jnp.max(maxima, axis=0)
    rescale = jnp.exp(maxima - joined[None])
    return (
        joined,
        jnp.sum(rescale * totals, axis=0),
        jnp.sum(rescale[..., None] * outputs, axis=0),
    )


def cache_partials(
    queries,
    page_block,
    page_item,
    tail_block,
    tail_owner,
    prefix_length,
    tail_length,
    row_index,
    slopes,
):
    cont_count = queries.shape[0]
    prompts = cont_count // CONT
    head_count = queries.shape[2]
    slot_count = page_block.shape[0]
    tokens = page_block.shape[2]
    token_index = row_index * tokens + jnp.arange(tokens, dtype=jnp.int32)
    step_index = jnp.arange(2, dtype=jnp.int32)
    slot_prompt = page_item // MAXPAGES
    slot_page = page_item % MAXPAGES
    by_prompt = queries.reshape(prompts, CONT * 2, head_count, HD)
    key_pos = slot_page[:, None] * PAGE + token_index[None, :]
    slot_len = prefix_length[slot_prompt]
    slot_tails = tail_length.reshape(prompts, CONT)[slot_prompt]
    query_pos = (
        slot_len[:, None, None] + slot_tails[:, :, None] + step_index[None, None, :]
    ).reshape(slot_count, CONT * 2)
    offset = (key_pos[:, None, :] - query_pos[:, :, None]).astype(jnp.float32)
    usable = jnp.broadcast_to((key_pos < slot_len[:, None])[:, None, :], offset.shape)
    page_keys = page_block[:, 0].reshape(slot_count, tokens, head_count, HD)
    page_values = page_block[:, 1].reshape(slot_count, tokens, head_count, HD)
    maxima, totals, outputs = slot_partials(
        by_prompt[slot_prompt], page_keys, page_values, usable, offset, slopes
    )
    prompt_max = (
        jnp.full((prompts, CONT * 2, head_count), masked_score, jnp.float32)
        .at[slot_prompt]
        .max(maxima)
    )
    rescale = jnp.exp(maxima - prompt_max[slot_prompt])
    prompt_total = (
        jnp.zeros((prompts, CONT * 2, head_count), jnp.float32)
        .at[slot_prompt]
        .add(rescale * totals)
    )
    prompt_out = (
        jnp.zeros((prompts, CONT * 2, head_count, HD), jnp.float32)
        .at[slot_prompt]
        .add(rescale[..., None] * outputs)
    )
    prefix_part = (
        prompt_max.reshape(cont_count, 2, head_count),
        prompt_total.reshape(cont_count, 2, head_count),
        prompt_out.reshape(cont_count, 2, head_count, HD),
    )
    tail_count = tail_block.shape[0]
    tail_lens = tail_length[tail_owner]
    tail_usable = jnp.broadcast_to(
        (token_index[None, :] < tail_lens[:, None])[:, None, :], (tail_count, 2, tokens)
    )
    tail_offset = (
        token_index[None, None, :] - tail_lens[:, None, None] - step_index[None, :, None]
    ).astype(jnp.float32)
    tail_keys = tail_block[:, 0].reshape(tail_count, tokens, head_count, HD)
    tail_values = tail_block[:, 1].reshape(tail_count, tokens, head_count, HD)
    tail_max, tail_total, tail_out = slot_partials(
        queries[tail_owner], tail_keys, tail_values, tail_usable, tail_offset, slopes
    )
    cont_max = (
        jnp.full((cont_count, 2, head_count), masked_score, jnp.float32)
        .at[tail_owner]
        .set(tail_max)
    )
    cont_total = jnp.zeros((cont_count, 2, head_count), jnp.float32).at[tail_owner].set(tail_total)
    cont_out = jnp.zeros((cont_count, 2, head_count, HD), jnp.float32).at[tail_owner].set(tail_out)
    return merge_pair(prefix_part, (cont_max, cont_total, cont_out))


def normalize(values, sum_one, sum_two, gain, shift):
    center = sum_one / D
    spread = sum_two / D - center * center
    return (
        (values - center[:, None])
        * lax.rsqrt(spread + norm_eps)[:, None]
        * gain.astype(jnp.float32)
        + shift.astype(jnp.float32)
    ).astype(jnp.bfloat16)


def shards(
    residual,
    fresh_qkv,
    prefix_pages,
    tail_pages,
    prefix_item,
    tail_item,
    prefix_length,
    tail_length,
    out_weight,
    out_bias,
    mlp_gain,
    mlp_shift,
    up_weight,
    up_bias,
    down_weight,
    down_bias,
    next_gain,
    next_shift,
    score_weight,
    qkv_weight,
    qkv_bias,
):
    group_index = lax.axis_index("pages")
    row_index = lax.axis_index("row")
    col_index = lax.axis_index("col")
    group_count = lax.axis_size("pages")
    cont_local = residual.shape[0]
    row_total = cont_local * 2
    share = residual.shape[2]
    head_count = fresh_qkv.shape[3] // HD
    slopes = head_slopes(col_index * head_count, head_count)
    fresh_rows = fresh_qkv.reshape(cont_local, 2, 3, head_count, HD)
    slot_count = prefix_pages.shape[0]
    tail_slots = tail_pages.shape[0]
    everyone = lax.all_gather(fresh_qkv[:, :, 0], "pages", axis=0, tiled=True)
    page_item = lax.dynamic_slice_in_dim(prefix_item, group_index * slot_count, slot_count)
    tail_owner = lax.dynamic_slice_in_dim(tail_item, group_index * tail_slots, tail_slots)
    maxima, totals, outputs = cache_partials(
        everyone.reshape(everyone.shape[0], 2, head_count, HD),
        prefix_pages,
        page_item,
        tail_pages,
        tail_owner,
        prefix_length,
        tail_length,
        row_index,
        slopes,
    )
    maxima, totals, outputs = (
        lax.all_to_all(
            maxima.reshape(group_count, row_total, head_count),
            "pages",
            split_axis=0,
            concat_axis=0,
            tiled=True,
        ),
        lax.all_to_all(
            totals.reshape(group_count, row_total, head_count),
            "pages",
            split_axis=0,
            concat_axis=0,
            tiled=True,
        ),
        lax.all_to_all(
            outputs.reshape(group_count, row_total, head_count, HD),
            "pages",
            split_axis=0,
            concat_axis=0,
            tiled=True,
        ),
    )
    cache_max, cache_total, cache_out = fold_sources(maxima, totals, outputs)
    cache_max, cache_total, cache_out = combined_all(
        (cache_max, cache_total, cache_out), "row", merge_pair
    )
    step_index = jnp.arange(2, dtype=jnp.int32)
    new_usable = jnp.broadcast_to(
        (step_index[None, :] <= step_index[:, None])[None], (cont_local, 2, 2)
    )
    new_offset = jnp.broadcast_to(
        (step_index[None, :] - step_index[:, None]).astype(jnp.float32)[None], (cont_local, 2, 2)
    )
    new_part = slot_partials(
        fresh_rows[:, :, 0],
        fresh_rows[:, :, 1],
        fresh_rows[:, :, 2],
        new_usable,
        new_offset,
        slopes,
    )
    joined_max, joined_total, joined_out = merge_pair(
        (
            cache_max.reshape(cont_local, 2, head_count),
            cache_total.reshape(cont_local, 2, head_count),
            cache_out.reshape(cont_local, 2, head_count, HD),
        ),
        new_part,
    )
    attended = (
        (joined_out / joined_total[..., None])
        .astype(jnp.bfloat16)
        .reshape(row_total, head_count * HD)
    )
    head_term = jnp.dot(attended, out_weight, preferred_element_type=jnp.float32)
    hidden_one = (
        residual.reshape(row_total, share).astype(jnp.float32)
        + lax.psum_scatter(head_term, "col", scatter_dimension=1, tiled=True)
        + out_bias.astype(jnp.float32)
    )
    gain_part = lax.dynamic_slice_in_dim(mlp_gain, col_index * share, share)
    shift_part = lax.dynamic_slice_in_dim(mlp_shift, col_index * share, share)
    sum_one, sum_two = lax.psum(
        (jnp.sum(hidden_one, axis=1), jnp.sum(hidden_one * hidden_one, axis=1)), ("row", "col")
    )
    normed_a = lax.all_gather(
        normalize(hidden_one, sum_one, sum_two, gain_part, shift_part), "col", axis=1, tiled=True
    )
    up_share = lax.psum_scatter(
        jnp.dot(normed_a, up_weight, preferred_element_type=jnp.float32),
        "row",
        scatter_dimension=1,
        tiled=True,
    )
    hidden_two = jax.nn.gelu(up_share + up_bias.astype(jnp.float32), approximate=True).astype(
        jnp.bfloat16
    )
    down_sum = jnp.dot(
        lax.all_gather(hidden_two, "row", axis=1, tiled=True),
        down_weight,
        preferred_element_type=jnp.float32,
    )
    down_share = lax.psum_scatter(
        down_sum.astype(jnp.bfloat16), "col", scatter_dimension=1, tiled=True
    ).astype(jnp.float32)
    layer_out = (hidden_one + down_share + down_bias.astype(jnp.float32)).astype(jnp.bfloat16)
    out_wide = layer_out.astype(jnp.float32)
    gain_part = lax.dynamic_slice_in_dim(next_gain, col_index * share, share)
    shift_part = lax.dynamic_slice_in_dim(next_shift, col_index * share, share)
    score_part = lax.dynamic_slice_in_dim(score_weight, col_index * share, share).astype(
        jnp.float32
    )
    sum_one, sum_two, score_sum = lax.psum(
        (
            jnp.sum(out_wide, axis=1),
            jnp.sum(out_wide * out_wide, axis=1),
            jnp.sum(out_wide * score_part, axis=1),
        ),
        ("row", "col"),
    )
    normed_b = lax.all_gather(
        normalize(out_wide, sum_one, sum_two, gain_part, shift_part), "col", axis=1, tiled=True
    )
    qkv_share = lax.psum_scatter(
        jnp.dot(normed_b, qkv_weight, preferred_element_type=jnp.float32).astype(jnp.bfloat16),
        "row",
        scatter_dimension=1,
        tiled=True,
    ).astype(jnp.float32)
    projected_next = (qkv_share + qkv_bias.astype(jnp.float32)).astype(jnp.bfloat16)
    return (
        layer_out.reshape(cont_local, 2, share),
        score_sum.reshape(cont_local, 2),
        projected_next.reshape(cont_local, 2, qkv_share.shape[1]),
    )


def solution(mesh):
    in_specs = (
        P("pages", None, ("row", "col")),
        P("pages", None, None, "col"),
        P("pages", None, "row", "col"),
        P("pages", None, "row", "col"),
        P(),
        P(),
        P(),
        P(),
        P("col", "row"),
        P(("row", "col")),
        P("row"),
        P("row"),
        P("row", "col"),
        P(("col", "row")),
        P("col", "row"),
        P(("row", "col")),
        P("row"),
        P("row"),
        P("row"),
        P("row", "col"),
        P(("col", "row")),
    )
    out_specs = (
        P("pages", None, ("row", "col")),
        P("pages", None),
        P("pages", None, ("col", "row")),
    )
    return jax.shard_map(shards, mesh=mesh, in_specs=in_specs, out_specs=out_specs, check_vma=False)
```

profile of v0, /device:TPU:2, one launch (start us, length us, event | category | flops | bytes accessed | tf_op | source)
XLA Modules:
  0.0 629.2 jit_solution(3406723916201025579)
XLA Ops:
  7.2 1.6 slice.33
  10.9 1.5 gather_fusion.3
  12.4 1.3 fusion.57
  19.9 35.8 %all-gather.9.cloned.1.call-done = bf16[512,2,1,512]{3,1,2,0:T(2,128)(2,1)} async-done(((bf16[32,2,1,512]{3,1,2,0:T(2,128)(2,1)}), bf16[512,2,1,512]{3,1,2,0:T(2,128)(2,1)}) %all-gather.9.cloned.1.call-update) | async-done | bytes 1048592 | tf_op jit(solution)/shard_map/all_gather | solution.py:195
  55.7 1.7 reshape_reshape.3
  57.7 1.4 gather_fusion.1
  59.1 1.5 fusion.61
  60.7 1.1 scatter_fusion
  62.6 1.5 reshape.233
  64.1 2.0 gather_fusion.4
  66.1 1.6 fusion.60
  70.2 1.1 scatter_fusion.2
  71.3 1.1 copy.151
  72.5 1.5 scatter_fusion.3
  74.2 1.5 scatter_fusion.1
  75.7 2.5 multiply_add_fusion
  78.2 1.3 copy.147
  80.2 4.6 all-to-all-start
  84.8 2.9 fusion.4
  89.6 2.6 scatter_fusion.4
  92.3 1.5 copy.158
  94.5 1.5 scatter_fusion.5
  96.0 7.2 %all-to-all-start.1 = ((f32[16,1,256]{2,1,0:T(1,128)}), f32[16,1,256]{2,1,0:T(1,128)S(1)}, u32[]{:S(2)}, u32[]{:S(2)}) async-start(f32[16,1,256]{2,1,0:T(1,128)} %reshape.385), calls=%async_computation.1 | async-start | bytes 32768 | tf_op jit(solution)/shard_map/all_to_all | solution.py:217
  103.2 6.1 fusion.3
  109.3 1.5 all-to-all-done.1
  110.8 5.7 all-to-all-start.2
  119.8 45.9 %all-to-all-done.2 = f32[16,64,4,128]{3,2,1,0:T(4,128)S(1)} async-done(((f32[16,64,4,128]{3,2,1,0:T(4,128)}), f32[16,64,4,128]{3,2,1,0:T(4,128)S(1)}, u32[]{:S(2)}, u32[]{:S(2)}) %all-to-all-start.2) | async-done | bytes 2097184 | tf_op jit(solution)/shard_map/all_to_all | solution.py:224
  165.7 2.9 multiply_reduce_fusion
  170.9 24.3 %all-gather.4 = f32[8,64,4]{1,2,0:T(4,128)S(1)} all-gather(f32[1,64,4]{1,2,0:T(4,128)S(1)} %copy.149), channel_id=3, replica_groups=mesh['pages'=16,'row'=8,'col'=4] {'row'}, dimensions={0}, use_global_device_ids=true | all-gather | bytes 9216 | tf_op jit(solution)/shard_map/all_gather | solution.py:18
  195.2 21.2 %all-gather.5 = f32[8,64,4]{1,2,0:T(4,128)S(1)} all-gather(f32[1,64,4]{1,2,0:T(4,128)S(1)} %copy.155), channel_id=4, replica_groups=mesh['pages'=16,'row'=8,'col'=4] {'row'}, dimensions={0}, use_global_device_ids=true | all-gather | bytes 9216 | tf_op jit(solution)/shard_map/all_gather | solution.py:18
  217.3 10.9 %while.19 = (s32[]{:T(128)}, f32[64,4]{0,1:T(4,128)S(1)}, f32[64,4]{0,1:T(4,128)S(1)}, f32[64,4,128]{2,1,0:T(4,128)S(1)}, f32[8,64,4]{1,2,0:T(4,128)S(1)}, /*ind...) while((s32[]{:T(128)}, f32[64,4]{0,1:T(4,128)S(1)}, ...), condition=%wide.region_14.15_spmd, body=%wide.region_13.14_spmd.sunk | while | flops 99845 | bytes 407703 | solution.py:24
  217.6 1.3 fusion.75
  219.1 1.3 fusion.75
  220.7 1.3 fusion.75
  222.2 1.3 fusion.75
  223.8 1.3 fusion.75
  225.4 1.3 fusion.75
  226.9 1.3 fusion.75
  230.1 20.7 %reduce-scatter.13.cloned.1.call-done = f32[64,64]{1,0:T(8,128)} async-done(((f32[256,64]{1,0:T(8,128)}), f32[64,64]{1,0:T(8,128)}) %reduce-scatter.13.cloned.1.call-update) | async-done | bytes 16400
  251.7 71.3 %all-reduce.1 = (f32[64]{0:T(128)S(1)}, f32[64]{0:T(128)S(1)}) all-reduce(f32[64]{0:T(128)S(1)} %get-tuple-element.200, f32[64]{0:T(128)S(1)} %get-tuple-element.199), channel_id=1, replica_groups=mesh['pages'=16,'row'=8,'col'=4] {'row','col'}, use_global_device_ids=true, to_apply=%region_21.22 | all-reduce | flops 128 | bytes 1024 | tf_op jit(solution)/shard_map/psum | solution.py:272
  323.2 12.8 %all_gather.37 = bf16[64,256]{0,1:T(8,128)(2,1)S(1)} all-gather(bf16[64,64]{0,1:T(8,128)(2,1)S(1)} %copy.179), channel_id=1, replica_groups=mesh['pages'=16,'row'=8,'col'=4] {'col'}, dimensions={1}, use_global_device_ids=true | all-gather | bytes 40960 | tf_op jit(solution)/shard_map/all_gather | solution.py:275
  336.1 1.1 fusion.63
  337.4 39.7 %reduce-scatter.11.cloned.1.call-done = f32[64,256]{1,0:T(8,128)} async-done(((f32[64,2048]{1,0:T(8,128)}), f32[64,256]{1,0:T(8,128)}) %reduce-scatter.11.cloned.1.call-update) | async-done | bytes 65552 | tf_op jit(solution)/shard_map/reduce_scatter | solution.py:278
  378.0 24.8 %all_gather.38 = bf16[64,2048]{1,0:T(8,128)(2,1)S(1)} all-gather(bf16[64,256]{1,0:T(8,128)(2,1)S(1)} %fusion.32), channel_id=1, replica_groups=mesh['pages'=16,'row'=8,'col'=4] {'row'}, dimensions={1}, use_global_device_ids=true | all-gather | bytes 294912 | tf_op jit(solution)/shard_map/all_gather | solution.py:288
  403.9 22.6 %reduce-scatter.15.cloned.1.call-done = bf16[64,64]{1,0:T(8,128)(2,1)} async-done(((bf16[256,64]{1,0:T(8,128)(2,1)}), bf16[64,64]{1,0:T(8,128)(2,1)}) %reduce-scatter.15.cloned.1.call-update) | async-done | bytes 8208
  427.6 138.0 %all-reduce = (f32[32,2]{1,0:T(8,128)S(1)}, f32[64]{0:T(128)S(1)}, f32[64]{0:T(128)S(1)}) all-reduce(f32[32,2]{1,0:T(8,128)S(1)} %reshape.245, f32[64]{0:T(128)S(1)} %get-tuple-element.202, f32[64]{0:T(128)S(1)} %get-tuple-element.201), channel_id=1, replica_groups=mesh['pages'=16,'row'=8,'col'=4] {'row','col'}, use_global_device_ids=true, to_apply=%region_25.26 | all-reduce | flops 192 | bytes 1536 | tf_op jit(solution)/shard_map/psum | solution.py:302
  565.8 14.2 %all_gather.39 = bf16[64,256]{0,1:T(8,128)(2,1)S(1)} all-gather(bf16[64,64]{0,1:T(8,128)(2,1)S(1)} %copy.180), channel_id=1, replica_groups=mesh['pages'=16,'row'=8,'col'=4] {'col'}, dimensions={1}, use_global_device_ids=true | all-gather | bytes 40960 | tf_op jit(solution)/shard_map/all_gather | solution.py:310
  581.9 38.9 %reduce-scatter.17.cloned.1.call-done = bf16[192,64]{1,0:T(8,128)(2,1)} async-done(((bf16[1536,64]{1,0:T(8,128)(2,1)}), bf16[192,64]{1,0:T(8,128)(2,1)}) %reduce-scatter.17.cloned.1.call-update) | async-done | bytes 24592
  (213 shorter events, 32.9 us)
Async XLA Ops:
  7.2 328.9 %copy-start = (bf16[256,2048]{1,0:T(8,128)(2,1)S(1)}, bf16[256,2048]{1,0:T(8,128)(2,1)}, u32[]{:S(2)}) copy-start(bf16[256,2048]{1,0:T(8,128)(2,1)} %param.35) | copy-start | bytes 3145732
  7.2 7.4 %copy-start.25 = (s32[256]{0:T(256)S(1)}, s32[256]{0:T(256)}, u32[]{:S(2)}) copy-start(s32[256]{0:T(256)} %param.27) | copy-start | bytes 3076
  7.2 8.1 %copy-start.1 = (s32[32]{0:T(128)S(1)}, s32[32]{0:T(128)}, u32[]{:S(2)}) copy-start(s32[32]{0:T(128)} %param.29) | copy-start | bytes 388
  7.2 48.5 %all-gather.9.cloned.1.call-start = ((), (), s32[]{:S(2)}) async-start(), calls=%async_computation.8 | async-start | bytes 1114112 | tf_op jit(solution)/shard_map/all_gather | solution.py:195
  9.6 0.5 copy-start.21
  10.2 0.8 copy-start.24
  10.9 5.5 copy-start.6
  14.8 55.5 %copy-start.19 = (s32[16]{0:T(128)}, s32[16]{0:T(128)S(1)}, u32[]{:S(2)}) copy-start(s32[16]{0:T(128)S(1)} %compare_select_fusion.1) | copy-start | bytes 196
  18.9 50.4 %copy-start.16 = (pred[16,16]{1,0:T(8,128)(4,1)}, pred[16,16]{1,0:T(8,128)(4,1)S(1)}, u32[]{:S(2)}) copy-start(pred[16,16]{1,0:T(8,128)(4,1)S(1)} %broadcast_compare_fusion.1) | copy-start | bytes 772
  19.0 49.6 %copy-start.17 = (pred[32,16]{1,0:T(8,128)(4,1)}, pred[32,16]{1,0:T(8,128)(4,1)S(1)}, u32[]{:S(2)}) copy-start(pred[32,16]{1,0:T(8,128)(4,1)S(1)} %broadcast_compare_fusion) | copy-start | bytes 1540
  57.7 4.9 copy-start.2
  66.1 6.4 %copy-start.22 = (s32[32]{0:T(128)S(1)}, s32[32]{0:T(128)}, u32[]{:S(2)}) copy-start(s32[32]{0:T(128)} %copy-done.21) | copy-start | bytes 388
  67.7 0.9 copy-start.13
  70.2 4.0 copy-start.12
  75.7 9.1 %copy-start.11 = (f32[8,32,8]{1,2,0:T(8,128)S(1)}, f32[8,32,8]{1,2,0:T(8,128)}, u32[]{:S(2)}) copy-start(f32[8,32,8]{1,2,0:T(8,128)} %get-tuple-element.270) | copy-start | bytes 24580
  78.2 9.5 %copy-start.7 = (bf16[32,16,4,128]{3,2,1,0:T(4,128)(2,1)S(1)}, bf16[32,16,4,128]{3,2,1,0:T(4,128)(2,1)}, u32[]{:S(2)}) copy-start(bf16[32,16,4,128]{3,2,1,0:T(4,128)(2,1)} %reshape_squeeze.15) | copy-start | bytes 1572868
  78.2 9.5 %copy-start.14 = (f32[32,2,4,16]{3,1,2,0:T(2,128)S(1)}, f32[32,2,4,16]{3,1,2,0:T(2,128)}, u32[]{:S(2)}) copy-start(f32[32,2,4,16]{3,1,2,0:T(2,128)} %copy-done.13) | copy-start | bytes 49156
  78.2 9.5 %copy-start.18 = (pred[32,16]{1,0:T(8,128)(4,1)S(1)}, pred[32,16]{1,0:T(8,128)(4,1)}, u32[]{:S(2)}) copy-start(pred[32,16]{1,0:T(8,128)(4,1)} %copy-done.17) | copy-start | bytes 1540
  79.5 8.9 %copy-start.3 = (f32[128,8,4]{2,1,0:T(8,128)S(1)}, f32[128,8,4]{2,1,0:T(8,128)}, u32[]{:S(2)}) copy-start(f32[128,8,4]{2,1,0:T(8,128)} %get-tuple-element.271) | copy-start | bytes 49156
  80.2 15.7 %all-to-all-start = ((f32[16,1,256]{2,1,0:T(1,128)}), f32[16,1,256]{2,1,0:T(1,128)S(1)}, u32[]{:S(2)}, u32[]{:S(2)}) async-start(f32[16,1,256]{2,1,0:T(1,128)} %reshape.383), calls=%async_computation | async-start | bytes 32768 | tf_op jit(solution)/shard_map/all_to_all | solution.py:210
  87.7 1.9 copy-start.20
  93.8 0.7 copy-start.23
  96.0 14.9 %all-to-all-start.1 = ((f32[16,1,256]{2,1,0:T(1,128)}), f32[16,1,256]{2,1,0:T(1,128)S(1)}, u32[]{:S(2)}, u32[]{:S(2)}) async-start(f32[16,1,256]{2,1,0:T(1,128)} %reshape.385), calls=%async_computation.1 | async-start | bytes 32768 | tf_op jit(solution)/shard_map/all_to_all | solution.py:217
  110.8 54.9 %all-to-all-start.2 = ((f32[16,64,4,128]{3,2,1,0:T(4,128)}), f32[16,64,4,128]{3,2,1,0:T(4,128)S(1)}, u32[]{:S(2)}, u32[]{:S(2)}) async-start(f32[16,64,4,128]{3,2,1,0:T(4,128)} %bitcast.145), calls=%async_computation.2 | async-start | bytes 4194304 | tf_op jit(solution)/shard_map/all_to_all | solution.py:224
  116.5 52.1 %copy-start.8 = (bf16[32,2,3,512]{3,1,2,0:T(2,128)(2,1)S(1)}, bf16[32,2,3,512]{3,1,2,0:T(2,128)(2,1)}, u32[]{:S(2)}) copy-start(bf16[32,2,3,512]{3,1,2,0:T(2,128)(2,1)} %param.24) | copy-start | bytes 589828
  116.5 99.8 %all-gather.11.cloned.1.call-start = ((), (), s32[]{:S(2)}) async-start(), calls=%async_computation.9 | async-start | bytes 1179648 | tf_op jit(solution)/shard_map/all_gather | solution.py:18
  118.7 50.2 %copy-start.35 = (f32[4]{0:T(128)S(1)}, f32[4]{0:T(128)}, u32[]{:S(2)}) copy-start(f32[4]{0:T(128)} %multiply_exponential_fusion) | copy-start | bytes 52
  168.6 82.1 %reduce-scatter.13.cloned.1.call-start = ((), (), s32[]{:S(2)}) async-start(), calls=%async_computation.10 | async-start | bytes 163840
  170.5 58.4 %copy-start.9 = (bf16[512,256]{1,0:T(8,128)(2,1)S(1)}, bf16[512,256]{1,0:T(8,128)(2,1)}, u32[]{:S(2)}) copy-start(bf16[512,256]{1,0:T(8,128)(2,1)} %param.31) | copy-start | bytes 786436
  217.3 12.7 %copy-start.30 = (bf16[64]{0:T(256)(128)(2,1)S(1)}, bf16[64]{0:T(256)(128)(2,1)}, u32[]{:S(2)}) copy-start(bf16[64]{0:T(256)(128)(2,1)} %param.32) | copy-start | bytes 388
  217.3 12.7 %copy-start.26 = (bf16[256]{0:T(256)(128)(2,1)S(1)}, bf16[256]{0:T(256)(128)(2,1)}, u32[]{:S(2)}) copy-start(bf16[256]{0:T(256)(128)(2,1)} %param.34) | copy-start | bytes 1540
  217.3 12.7 %copy-start.27 = (bf16[256]{0:T(256)(128)(2,1)S(1)}, bf16[256]{0:T(256)(128)(2,1)}, u32[]{:S(2)}) copy-start(bf16[256]{0:T(256)(128)(2,1)} %param.33) | copy-start | bytes 1540
  217.3 34.3 %copy-start.10 = (bf16[32,2,64]{2,1,0:T(2,128)(2,1)S(1)}, bf16[32,2,64]{2,1,0:T(2,128)(2,1)}, u32[]{:S(2)}) copy-start(bf16[32,2,64]{2,1,0:T(2,128)(2,1)} %param.23) | copy-start | bytes 24580
  228.3 109.0 %copy-start.31 = (bf16[64]{0:T(256)(128)(2,1)S(1)}, bf16[64]{0:T(256)(128)(2,1)}, u32[]{:S(2)}) copy-start(bf16[64]{0:T(256)(128)(2,1)} %param.38) | copy-start | bytes 388
  228.3 109.0 %copy-start.32 = (bf16[256]{0:T(256)(128)(2,1)S(1)}, bf16[256]{0:T(256)(128)(2,1)}, u32[]{:S(2)}) copy-start(bf16[256]{0:T(256)(128)(2,1)} %param.36) | copy-start | bytes 1540
  228.3 109.0 %copy-start.28 = (bf16[256]{0:T(256)(128)(2,1)S(1)}, bf16[256]{0:T(256)(128)(2,1)}, u32[]{:S(2)}) copy-start(bf16[256]{0:T(256)(128)(2,1)} %param.40) | copy-start | bytes 1540
  228.3 109.0 %copy-start.29 = (bf16[256]{0:T(256)(128)(2,1)S(1)}, bf16[256]{0:T(256)(128)(2,1)}, u32[]{:S(2)}) copy-start(bf16[256]{0:T(256)(128)(2,1)} %param.39) | copy-start | bytes 1540
  228.3 174.5 %copy-start.4 = (bf16[2048,256]{1,0:T(8,128)(2,1)S(1)}, bf16[2048,256]{1,0:T(8,128)(2,1)}, u32[]{:S(2)}) copy-start(bf16[2048,256]{1,0:T(8,128)(2,1)} %param.37) | copy-start | bytes 3145732
  229.9 147.2 %reduce-scatter.11.cloned.1.call-start = ((), (), s32[]{:S(2)}) async-start(), calls=%async_computation.7 | async-start | bytes 589824 | tf_op jit(solution)/shard_map/reduce_scatter | solution.py:278
  323.1 80.7 %copy-start.33 = (bf16[256]{0:T(256)(128)(2,1)S(1)}, bf16[256]{0:T(256)(128)(2,1)}, u32[]{:S(2)}) copy-start(bf16[256]{0:T(256)(128)(2,1)} %param.41) | copy-start | bytes 1540
  336.1 244.0 %copy-start.5 = (bf16[256,1536]{1,0:T(8,128)(2,1)S(1)}, bf16[256,1536]{1,0:T(8,128)(2,1)}, u32[]{:S(2)}) copy-start(bf16[256,1536]{1,0:T(8,128)(2,1)} %param.42) | copy-start | bytes 2359300
  337.2 89.3 %reduce-scatter.15.cloned.1.call-start = ((), (), s32[]{:S(2)}) async-start(), calls=%async_computation.11 | async-start | bytes 81920
  377.9 203.3 %copy-start.34 = (bf16[192]{0:T(256)(128)(2,1)S(1)}, bf16[192]{0:T(256)(128)(2,1)}, u32[]{:S(2)}) copy-start(bf16[192]{0:T(256)(128)(2,1)} %param.43) | copy-start | bytes 1156
  403.8 217.0 %reduce-scatter.17.cloned.1.call-start = ((), (), s32[]{:S(2)}) async-start(), calls=%async_computation.12 | async-start | bytes 442368
  427.5 194.9 %copy-start.15 = (bf16[64,64]{1,0:T(8,128)(2,1)}, bf16[64,64]{1,0:T(8,128)(2,1)S(1)}, u32[]{:S(2)}) copy-start(bf16[64,64]{1,0:T(8,128)(2,1)S(1)} %get-tuple-element.227) | copy-start | bytes 24580
Sparse Core Ops, SparseCore 0:
  10.2 45.5 all-gather.8
  168.7 41.4 all-gather.10
  230.0 20.6 reduce-scatter.12
  337.3 39.6 reduce-scatter.10
  403.9 22.5 reduce-scatter.14
  581.4 39.4 reduce-scatter.16
where the time goes:
time: 630 us; the launch traced here: 629 us
  blocking collectives  307 us (49%)
  waiting for transfers between devices  205 us (33%)
  local copies, waits for them, and re-layouts  40.9 us (6%)
  other arithmetic  33.2 us (5%)
  starting transfers between devices  17.7 us (3%)
  between operations  14.9 us (2%)
  matrix products  10.4 us (2%)
    psum x1, blocking collectives, shards(): lax.psum((jnp.sum(out_wide, axis=1), jnp.sum(out_wide * out_wide, axis=1)...  138 us
    unnamed x9, waiting for transfers between devices  82.3 us
    psum x1, blocking collectives, shards(): lax.psum((jnp.sum(hidden_one, axis=1), jnp.sum(hidden_one * hidden_one, a...  71.3 us
    all_to_all x1, waiting for transfers between devices, shards(): lax.all_to_all(outputs.reshape(group_count, row_total, head_count, HD), '...  45.9 us
    all_gather x2, blocking collectives, combined_all(): everything = jax.tree.map(lambda part: lax.all_gather(part, axis), shard)  45.5 us
    reduce_scatter x1, waiting for transfers between devices, shards(): lax.psum_scatter(jnp.dot(normed_a, up_weight, preferred_element_type=jnp....  39.7 us
    all_gather x1, waiting for transfers between devices, shards(): everyone = lax.all_gather(fresh_qkv[:, :, 0], 'pages', axis=0, tiled=True)  35.8 us
    all_gather x1, blocking collectives, shards(): lax.all_gather(hidden_two, 'row', axis=1, tiled=True)  24.8 us
  transfers between devices with their start and end apart: 9, of which 7 were waited for; matrix products, arithmetic and copies ran while one was open for 5% of the time, Pallas kernels for 0%

commit v1 on v0

--- a/solution.py
+++ b/solution.py
@@ -299,13 +299,20 @@
     score_part = lax.dynamic_slice_in_dim(score_weight, col_index * share, share).astype(
         jnp.float32
     )
-    sum_one, sum_two, score_sum = lax.psum(
+
+    def attach_clusters_for(vals):
+        ax_name = "col"
+        which_axis = "row"
+        for kk in (which_axis, ax_name):
+            vals = lax.psum(vals, kk)
+        return vals
+
+    sum_one, sum_two, score_sum = attach_clusters_for(
         (
             jnp.sum(out_wide, axis=1),
             jnp.sum(out_wide * out_wide, axis=1),
             jnp.sum(out_wide * score_part, axis=1),
-        ),
-        ("row", "col"),
+        )
     )
     normed_b = lax.all_gather(
         normalize(out_wide, sum_one, sum_two, gain_part, shift_part), "col", axis=1, tiled=True

time: 630 us -> 522 us (0.83)
  the two profiles are of different devices: /device:TPU:2 before, /device:TPU:4 now
where the time goes in v1:
time: 522 us; the launch traced here: 521 us
  waiting for transfers between devices  203 us (39%)
  blocking collectives  201 us (39%)
  local copies, waits for them, and re-layouts  40.9 us (8%)
  other arithmetic  33.2 us (6%)
  starting transfers between devices  17.7 us (3%)
  between operations  14.9 us (3%)
  matrix products  10.4 us (2%)
    unnamed x9, waiting for transfers between devices  80.7 us
    psum x1, blocking collectives, shards(): lax.psum((jnp.sum(hidden_one, axis=1), jnp.sum(hidden_one * hidden_one, a...  71.1 us
    all_to_all x1, waiting for transfers between devices, shards(): lax.all_to_all(outputs.reshape(group_count, row_total, head_count, HD), '...  45.9 us
    all_gather x2, blocking collectives, combined_all(): everything = jax.tree.map(lambda part: lax.all_gather(part, axis), shard)  45.5 us
    reduce_scatter x1, waiting for transfers between devices, shards(): lax.psum_scatter(jnp.dot(normed_a, up_weight, preferred_element_type=jnp....  38.5 us
    all_gather x1, waiting for transfers between devices, shards(): everyone = lax.all_gather(fresh_qkv[:, :, 0], 'pages', axis=0, tiled=True)  35.9 us
    psum x2, blocking collectives, attach_clusters_for(): vals = lax.psum(vals, kk)  33.2 us
    all_gather x1, blocking collectives, shards(): lax.all_gather(hidden_two, 'row', axis=1, tiled=True)  24.8 us
  transfers between devices with their start and end apart: 9, of which 7 were waited for; matrix products, arithmetic and copies ran while one was open for 6% of the time, Pallas kernels for 0%

profile of v1, /device:TPU:4, one launch (start us, length us, event | category | flops | bytes accessed | tf_op | source)
XLA Modules:
  0.0 520.9 jit_solution(8959349826260653352)
XLA Ops:
  7.2 1.6 slice.33
  10.9 1.5 gather_fusion.3
  12.4 1.3 fusion.57
  19.8 35.9 %all-gather.9.cloned.1.call-done = bf16[512,2,1,512]{3,1,2,0:T(2,128)(2,1)} async-done(((bf16[32,2,1,512]{3,1,2,0:T(2,128)(2,1)}), bf16[512,2,1,512]{3,1,2,0:T(2,128)(2,1)}) %all-gather.9.cloned.1.call-update) | async-done | bytes 1048592 | tf_op jit(solution)/shard_map/all_gather | solution.py:195
  55.7 1.7 reshape_reshape.3
  57.6 1.4 gather_fusion.1
  59.1 1.5 fusion.61
  60.6 1.1 scatter_fusion
  62.6 1.5 reshape.233
  64.1 2.0 gather_fusion.4
  66.1 1.5 fusion.60
  70.2 1.1 scatter_fusion.2
  72.5 1.5 scatter_fusion.3
  74.1 1.5 scatter_fusion.1
  75.6 2.5 multiply_add_fusion
  78.1 1.3 copy.147
  80.2 4.6 all-to-all-start
  84.8 2.9 fusion.4
  89.6 2.6 scatter_fusion.4
  92.2 1.5 copy.158
  94.4 1.5 scatter_fusion.5
  95.9 7.2 %all-to-all-start.1 = ((f32[16,1,256]{2,1,0:T(1,128)}), f32[16,1,256]{2,1,0:T(1,128)S(1)}, u32[]{:S(2)}, u32[]{:S(2)}) async-start(f32[16,1,256]{2,1,0:T(1,128)} %reshape.385), calls=%async_computation.1 | async-start | bytes 32768 | tf_op jit(solution)/shard_map/all_to_all | solution.py:217
  103.2 6.1 %fusion.3 = f32[512,2,4,128]{3,2,1,0:T(4,128)} fusion(f32[512,2,4,128]{3,1,0,2:T(2,128)} %bitcast.146, f32[512,2,4,128]{3,2,1,0:T(4,128)S(1)} %scatter_fusion.5, f32[512,2,4]{2,1,0:T(2,128)} %bitcast.154, f32[512,2,4]{2,1,0:T(2,128)} %bitcast.153), kind=kLoop, calls=%fused_computation.22 | loop fusion | flops 1572864 | bytes 6324224 | tf_op jit(solution)/shard_map/add | solution.py:57
  109.3 1.5 all-to-all-done.1
  110.8 5.7 %all-to-all-start.2 = ((f32[16,64,4,128]{3,2,1,0:T(4,128)}), f32[16,64,4,128]{3,2,1,0:T(4,128)S(1)}, u32[]{:S(2)}, u32[]{:S(2)}) async-start(f32[16,64,4,128]{3,2,1,0:T(4,128)} %bitcast.145), calls=%async_computation.2 | async-start | bytes 4194304 | tf_op jit(solution)/shard_map/all_to_all | solution.py:224
  119.7 45.9 %all-to-all-done.2 = f32[16,64,4,128]{3,2,1,0:T(4,128)S(1)} async-done(((f32[16,64,4,128]{3,2,1,0:T(4,128)}), f32[16,64,4,128]{3,2,1,0:T(4,128)S(1)}, u32[]{:S(2)}, u32[]{:S(2)}) %all-to-all-start.2) | async-done | bytes 2097184 | tf_op jit(solution)/shard_map/all_to_all | solution.py:224
  165.7 2.9 multiply_reduce_fusion
  170.8 24.3 %all-gather.4 = f32[8,64,4]{1,2,0:T(4,128)S(1)} all-gather(f32[1,64,4]{1,2,0:T(4,128)S(1)} %copy.149), channel_id=3, replica_groups=mesh['pages'=16,'row'=8,'col'=4] {'row'}, dimensions={0}, use_global_device_ids=true | all-gather | bytes 9216 | tf_op jit(solution)/shard_map/all_gather | solution.py:18
  195.1 21.2 %all-gather.5 = f32[8,64,4]{1,2,0:T(4,128)S(1)} all-gather(f32[1,64,4]{1,2,0:T(4,128)S(1)} %copy.155), channel_id=4, replica_groups=mesh['pages'=16,'row'=8,'col'=4] {'row'}, dimensions={0}, use_global_device_ids=true | all-gather | bytes 9216 | tf_op jit(solution)/shard_map/all_gather | solution.py:18
  217.3 10.9 %while.19 = (s32[]{:T(128)}, f32[64,4]{0,1:T(4,128)S(1)}, f32[64,4]{0,1:T(4,128)S(1)}, f32[64,4,128]{2,1,0:T(4,128)S(1)}, f32[8,64,4]{1,2,0:T(4,128)S(1)}, /*ind...) while((s32[]{:T(128)}, f32[64,4]{0,1:T(4,128)S(1)}, ...), condition=%wide.region_14.15_spmd, body=%wide.region_13.14_spmd.sunk | while | flops 99845 | bytes 407703 | solution.py:24
  217.5 1.3 fusion.75
  219.1 1.3 fusion.75
  220.6 1.3 fusion.75
  222.2 1.3 fusion.75
  223.8 1.3 fusion.75
  225.3 1.3 fusion.75
  226.9 1.3 fusion.75
  230.0 20.3 %reduce-scatter.13.cloned.1.call-done = f32[64,64]{1,0:T(8,128)} async-done(((f32[256,64]{1,0:T(8,128)}), f32[64,64]{1,0:T(8,128)}) %reduce-scatter.13.cloned.1.call-update) | async-done | bytes 16400
  251.2 71.1 %all-reduce = (f32[64]{0:T(128)S(1)}, f32[64]{0:T(128)S(1)}) all-reduce(f32[64]{0:T(128)S(1)} %get-tuple-element.200, f32[64]{0:T(128)S(1)} %get-tuple-element.199), channel_id=1, replica_groups=mesh['pages'=16,'row'=8,'col'=4] {'row','col'}, use_global_device_ids=true, to_apply=%region_21.22 | all-reduce | flops 128 | bytes 1024 | tf_op jit(solution)/shard_map/psum | solution.py:272
  322.6 14.6 %all_gather.37 = bf16[64,256]{0,1:T(8,128)(2,1)S(1)} all-gather(bf16[64,64]{0,1:T(8,128)(2,1)S(1)} %copy.179), channel_id=1, replica_groups=mesh['pages'=16,'row'=8,'col'=4] {'col'}, dimensions={1}, use_global_device_ids=true | all-gather | bytes 40960 | tf_op jit(solution)/shard_map/all_gather | solution.py:275
  337.2 1.1 fusion.63
  338.5 38.5 %reduce-scatter.11.cloned.1.call-done = f32[64,256]{1,0:T(8,128)} async-done(((f32[64,2048]{1,0:T(8,128)}), f32[64,256]{1,0:T(8,128)}) %reduce-scatter.11.cloned.1.call-update) | async-done | bytes 65552 | tf_op jit(solution)/shard_map/reduce_scatter | solution.py:278
  377.9 24.8 %all_gather.38 = bf16[64,2048]{1,0:T(8,128)(2,1)S(1)} all-gather(bf16[64,256]{1,0:T(8,128)(2,1)S(1)} %fusion.32), channel_id=1, replica_groups=mesh['pages'=16,'row'=8,'col'=4] {'row'}, dimensions={1}, use_global_device_ids=true | all-gather | bytes 294912 | tf_op jit(solution)/shard_map/all_gather | solution.py:288
  403.8 22.3 %reduce-scatter.15.cloned.1.call-done = bf16[64,64]{1,0:T(8,128)(2,1)} async-done(((bf16[256,64]{1,0:T(8,128)(2,1)}), bf16[64,64]{1,0:T(8,128)(2,1)}) %reduce-scatter.15.cloned.1.call-update) | async-done | bytes 8208
  427.1 18.1 %all-reduce.1 = (f32[64]{0:T(128)S(1)}, f32[64]{0:T(128)S(1)}, f32[64]{0:T(128)S(1)}) all-reduce(f32[64]{0:T(128)S(1)} %get-tuple-element.203, f32[64]{0:T(128)S(1)} %get-tuple-element.202, f32[64]{0:T(128)S(1)} %get-tuple-element.201), channel_id=1, replica_groups=mesh['pages'=16,'row'=8,'col'=4] {'row'}, use_global_device_ids=true, to_apply=%region_25.26 | all-reduce | flops 192 | bytes 1536 | tf_op jit(solution)/shard_map/psum | solution.py:307
  445.3 15.2 %all-reduce.2 = (f32[32,2]{1,0:T(8,128)S(1)}, f32[64]{0:T(128)S(1)}, f32[64]{0:T(128)S(1)}) all-reduce(f32[32,2]{1,0:T(8,128)S(1)} %reshape.245, f32[64]{0:T(128)S(1)} %get-tuple-element.221, f32[64]{0:T(128)S(1)} %get-tuple-element.222), channel_id=1, replica_groups=mesh['pages'=16,'row'=8,'col'=4] {'col'}, use_global_device_ids=true, to_apply=%region_26.27 | all-reduce | flops 192 | bytes 1536 | tf_op jit(solution)/shard_map/psum | solution.py:307
  460.6 11.9 %all_gather.39 = bf16[64,256]{0,1:T(8,128)(2,1)S(1)} all-gather(bf16[64,64]{0,1:T(8,128)(2,1)S(1)} %copy.180), channel_id=1, replica_groups=mesh['pages'=16,'row'=8,'col'=4] {'col'}, dimensions={1}, use_global_device_ids=true | all-gather | bytes 40960 | tf_op jit(solution)/shard_map/all_gather | solution.py:317
  474.4 38.1 %reduce-scatter.17.cloned.1.call-done = bf16[192,64]{1,0:T(8,128)(2,1)} async-done(((bf16[1536,64]{1,0:T(8,128)(2,1)}), bf16[192,64]{1,0:T(8,128)(2,1)}) %reduce-scatter.17.cloned.1.call-update) | async-done | bytes 24592
  (214 shorter events, 33.9 us)
Async XLA Ops:
  7.2 330.0 %copy-start = (bf16[256,2048]{1,0:T(8,128)(2,1)S(1)}, bf16[256,2048]{1,0:T(8,128)(2,1)}, u32[]{:S(2)}) copy-start(bf16[256,2048]{1,0:T(8,128)(2,1)} %param.35) | copy-start | bytes 3145732
  7.2 7.4 %copy-start.25 = (s32[256]{0:T(256)S(1)}, s32[256]{0:T(256)}, u32[]{:S(2)}) copy-start(s32[256]{0:T(256)} %param.27) | copy-start | bytes 3076
  7.2 8.1 %copy-start.1 = (s32[32]{0:T(128)S(1)}, s32[32]{0:T(128)}, u32[]{:S(2)}) copy-start(s32[32]{0:T(128)} %param.29) | copy-start | bytes 388
  7.2 48.5 %all-gather.9.cloned.1.call-start = ((), (), s32[]{:S(2)}) async-start(), calls=%async_computation.8 | async-start | bytes 1114112 | tf_op jit(solution)/shard_map/all_gather | solution.py:195
  9.6 0.5 copy-start.21
  10.1 0.8 copy-start.24
  10.9 5.5 %copy-start.6 = (bf16[16,2,16,512]{3,2,1,0:T(8,128)(2,1)S(1)}, bf16[16,2,16,512]{3,2,1,0:T(8,128)(2,1)}, u32[]{:S(2)}) copy-start(bf16[16,2,16,512]{3,2,1,0:T(8,128)(2,1)} %param.25) | copy-start | bytes 1572868
  14.7 55.4 %copy-start.19 = (s32[16]{0:T(128)}, s32[16]{0:T(128)S(1)}, u32[]{:S(2)}) copy-start(s32[16]{0:T(128)S(1)} %compare_select_fusion.1) | copy-start | bytes 196
  18.9 50.4 %copy-start.16 = (pred[16,16]{1,0:T(8,128)(4,1)}, pred[16,16]{1,0:T(8,128)(4,1)S(1)}, u32[]{:S(2)}) copy-start(pred[16,16]{1,0:T(8,128)(4,1)S(1)} %broadcast_compare_fusion.1) | copy-start | bytes 772
  18.9 49.6 %copy-start.17 = (pred[32,16]{1,0:T(8,128)(4,1)}, pred[32,16]{1,0:T(8,128)(4,1)S(1)}, u32[]{:S(2)}) copy-start(pred[32,16]{1,0:T(8,128)(4,1)S(1)} %broadcast_compare_fusion) | copy-start | bytes 1540
  57.6 4.9 copy-start.2
  66.1 6.4 %copy-start.22 = (s32[32]{0:T(128)S(1)}, s32[32]{0:T(128)}, u32[]{:S(2)}) copy-start(s32[32]{0:T(128)} %copy-done.21) | copy-start | bytes 388
  67.6 0.9 copy-start.13
  70.1 4.0 copy-start.12
  75.6 9.1 %copy-start.11 = (f32[8,32,8]{1,2,0:T(8,128)S(1)}, f32[8,32,8]{1,2,0:T(8,128)}, u32[]{:S(2)}) copy-start(f32[8,32,8]{1,2,0:T(8,128)} %get-tuple-element.273) | copy-start | bytes 24580
  78.1 9.6 %copy-start.7 = (bf16[32,16,4,128]{3,2,1,0:T(4,128)(2,1)S(1)}, bf16[32,16,4,128]{3,2,1,0:T(4,128)(2,1)}, u32[]{:S(2)}) copy-start(bf16[32,16,4,128]{3,2,1,0:T(4,128)(2,1)} %reshape_squeeze.15) | copy-start | bytes 1572868
  78.1 9.6 %copy-start.14 = (f32[32,2,4,16]{3,1,2,0:T(2,128)S(1)}, f32[32,2,4,16]{3,1,2,0:T(2,128)}, u32[]{:S(2)}) copy-start(f32[32,2,4,16]{3,1,2,0:T(2,128)} %copy-done.13) | copy-start | bytes 49156
  78.1 9.6 %copy-start.18 = (pred[32,16]{1,0:T(8,128)(4,1)S(1)}, pred[32,16]{1,0:T(8,128)(4,1)}, u32[]{:S(2)}) copy-start(pred[32,16]{1,0:T(8,128)(4,1)} %copy-done.17) | copy-start | bytes 1540
  79.5 8.9 %copy-start.3 = (f32[128,8,4]{2,1,0:T(8,128)S(1)}, f32[128,8,4]{2,1,0:T(8,128)}, u32[]{:S(2)}) copy-start(f32[128,8,4]{2,1,0:T(8,128)} %get-tuple-element.274) | copy-start | bytes 49156
  80.2 15.7 %all-to-all-start = ((f32[16,1,256]{2,1,0:T(1,128)}), f32[16,1,256]{2,1,0:T(1,128)S(1)}, u32[]{:S(2)}, u32[]{:S(2)}) async-start(f32[16,1,256]{2,1,0:T(1,128)} %reshape.383), calls=%async_computation | async-start | bytes 32768 | tf_op jit(solution)/shard_map/all_to_all | solution.py:210
  87.7 1.9 copy-start.20
  93.7 0.7 copy-start.23
  95.9 14.9 %all-to-all-start.1 = ((f32[16,1,256]{2,1,0:T(1,128)}), f32[16,1,256]{2,1,0:T(1,128)S(1)}, u32[]{:S(2)}, u32[]{:S(2)}) async-start(f32[16,1,256]{2,1,0:T(1,128)} %reshape.385), calls=%async_computation.1 | async-start | bytes 32768 | tf_op jit(solution)/shard_map/all_to_all | solution.py:217
  110.8 54.9 %all-to-all-start.2 = ((f32[16,64,4,128]{3,2,1,0:T(4,128)}), f32[16,64,4,128]{3,2,1,0:T(4,128)S(1)}, u32[]{:S(2)}, u32[]{:S(2)}) async-start(f32[16,64,4,128]{3,2,1,0:T(4,128)} %bitcast.145), calls=%async_computation.2 | async-start | bytes 4194304 | tf_op jit(solution)/shard_map/all_to_all | solution.py:224
  116.5 52.1 %copy-start.8 = (bf16[32,2,3,512]{3,1,2,0:T(2,128)(2,1)S(1)}, bf16[32,2,3,512]{3,1,2,0:T(2,128)(2,1)}, u32[]{:S(2)}) copy-start(bf16[32,2,3,512]{3,1,2,0:T(2,128)(2,1)} %param.24) | copy-start | bytes 589828
  116.5 99.8 %all-gather.11.cloned.1.call-start = ((), (), s32[]{:S(2)}) async-start(), calls=%async_computation.9 | async-start | bytes 1179648 | tf_op jit(solution)/shard_map/all_gather | solution.py:18
  118.7 50.2 %copy-start.35 = (f32[4]{0:T(128)S(1)}, f32[4]{0:T(128)}, u32[]{:S(2)}) copy-start(f32[4]{0:T(128)} %multiply_exponential_fusion) | copy-start | bytes 52
  168.6 81.7 %reduce-scatter.13.cloned.1.call-start = ((), (), s32[]{:S(2)}) async-start(), calls=%async_computation.10 | async-start | bytes 163840
  170.5 58.4 %copy-start.9 = (bf16[512,256]{1,0:T(8,128)(2,1)S(1)}, bf16[512,256]{1,0:T(8,128)(2,1)}, u32[]{:S(2)}) copy-start(bf16[512,256]{1,0:T(8,128)(2,1)} %param.31) | copy-start | bytes 786436
  217.2 12.7 %copy-start.30 = (bf16[64]{0:T(256)(128)(2,1)S(1)}, bf16[64]{0:T(256)(128)(2,1)}, u32[]{:S(2)}) copy-start(bf16[64]{0:T(256)(128)(2,1)} %param.32) | copy-start | bytes 388
  217.2 12.7 %copy-start.26 = (bf16[256]{0:T(256)(128)(2,1)S(1)}, bf16[256]{0:T(256)(128)(2,1)}, u32[]{:S(2)}) copy-start(bf16[256]{0:T(256)(128)(2,1)} %param.34) | copy-start | bytes 1540
  217.3 12.7 %copy-start.27 = (bf16[256]{0:T(256)(128)(2,1)S(1)}, bf16[256]{0:T(256)(128)(2,1)}, u32[]{:S(2)}) copy-start(bf16[256]{0:T(256)(128)(2,1)} %param.33) | copy-start | bytes 1540
  217.3 33.8 %copy-start.10 = (bf16[32,2,64]{2,1,0:T(2,128)(2,1)S(1)}, bf16[32,2,64]{2,1,0:T(2,128)(2,1)}, u32[]{:S(2)}) copy-start(bf16[32,2,64]{2,1,0:T(2,128)(2,1)} %param.23) | copy-start | bytes 24580
  228.2 110.2 %copy-start.31 = (bf16[64]{0:T(256)(128)(2,1)S(1)}, bf16[64]{0:T(256)(128)(2,1)}, u32[]{:S(2)}) copy-start(bf16[64]{0:T(256)(128)(2,1)} %param.38) | copy-start | bytes 388
  228.2 110.2 %copy-start.32 = (bf16[256]{0:T(256)(128)(2,1)S(1)}, bf16[256]{0:T(256)(128)(2,1)}, u32[]{:S(2)}) copy-start(bf16[256]{0:T(256)(128)(2,1)} %param.36) | copy-start | bytes 1540
  228.2 110.2 %copy-start.28 = (bf16[256]{0:T(256)(128)(2,1)S(1)}, bf16[256]{0:T(256)(128)(2,1)}, u32[]{:S(2)}) copy-start(bf16[256]{0:T(256)(128)(2,1)} %param.40) | copy-start | bytes 1540
  228.2 110.2 %copy-start.29 = (bf16[256]{0:T(256)(128)(2,1)S(1)}, bf16[256]{0:T(256)(128)(2,1)}, u32[]{:S(2)}) copy-start(bf16[256]{0:T(256)(128)(2,1)} %param.39) | copy-start | bytes 1540
  228.3 174.4 %copy-start.4 = (bf16[2048,256]{1,0:T(8,128)(2,1)S(1)}, bf16[2048,256]{1,0:T(8,128)(2,1)}, u32[]{:S(2)}) copy-start(bf16[2048,256]{1,0:T(8,128)(2,1)} %param.37) | copy-start | bytes 3145732
  229.8 147.1 %reduce-scatter.11.cloned.1.call-start = ((), (), s32[]{:S(2)}) async-start(), calls=%async_computation.7 | async-start | bytes 589824 | tf_op jit(solution)/shard_map/reduce_scatter | solution.py:278
  322.5 81.3 %copy-start.33 = (bf16[256]{0:T(256)(128)(2,1)S(1)}, bf16[256]{0:T(256)(128)(2,1)}, u32[]{:S(2)}) copy-start(bf16[256]{0:T(256)(128)(2,1)} %param.41) | copy-start | bytes 1540
  337.2 135.3 %copy-start.5 = (bf16[256,1536]{1,0:T(8,128)(2,1)S(1)}, bf16[256,1536]{1,0:T(8,128)(2,1)}, u32[]{:S(2)}) copy-start(bf16[256,1536]{1,0:T(8,128)(2,1)} %param.42) | copy-start | bytes 2359300
  338.3 87.8 %reduce-scatter.15.cloned.1.call-start = ((), (), s32[]{:S(2)}) async-start(), calls=%async_computation.11 | async-start | bytes 81920
  377.8 95.9 %copy-start.34 = (bf16[192]{0:T(256)(128)(2,1)S(1)}, bf16[192]{0:T(256)(128)(2,1)}, u32[]{:S(2)}) copy-start(bf16[192]{0:T(256)(128)(2,1)} %param.43) | copy-start | bytes 1156
  403.7 108.8 %reduce-scatter.17.cloned.1.call-start = ((), (), s32[]{:S(2)}) async-start(), calls=%async_computation.12 | async-start | bytes 442368
  427.1 86.9 %copy-start.15 = (bf16[64,64]{1,0:T(8,128)(2,1)}, bf16[64,64]{1,0:T(8,128)(2,1)S(1)}, u32[]{:S(2)}) copy-start(bf16[64,64]{1,0:T(8,128)(2,1)S(1)} %get-tuple-element.230) | copy-start | bytes 24580
Sparse Core Ops, SparseCore 0:
  10.2 45.4 all-gather.8
  168.7 41.4 all-gather.10
  230.0 20.2 reduce-scatter.12
  338.4 38.4 reduce-scatter.10
  403.8 22.2 reduce-scatter.14
  473.8 38.5 reduce-scatter.16
